TPU v7x, 32 devices: a whole 2x2x4 slice. The times are simulated.
32 devices in a mesh: grp: 1, seq: 8 (over z, y), head: 4 (over x, core).
Axes of the slice: x: 2, y: 2, z: 4, core: 2. Of those that a mesh axis runs over, the one named last changes fastest.
Arguments:
- ssm_values: bfloat16 [2048, 4096], P(('grp', 'seq'), 'head'), may hold values from -6 to 6
- ssm_gate: bfloat16 [2048, 4096], P(('grp', 'seq'), 'head'), may hold values from -6 to 6
- write_proj: bfloat16 [2048, 1024], P(('grp', 'seq'), 'head'), may hold values from -2.5 to 2.5
- read_proj: bfloat16 [2048, 1024], P(('grp', 'seq'), 'head'), may hold values from -2.5 to 2.5
- step_size: float32 [2048, 64], P(('grp', 'seq'), 'head'), may hold values from 0.003125 to 0.2
- decay_power: int32 [64], P('head'), may hold values from 0 to 15
- skip_gain: float32 [64], P('head'), may hold values from 0.5 to 1.5
- norm_gain: float32 [4096], P('head'), may hold values from 0.1 to 1.9
- out_weight: bfloat16 [4096, 2688], P('head', 'seq'), may hold values from -0.09375 to 0.09375
- residual: bfloat16 [2048, 2688], P(('grp', 'seq', 'head')), may hold values from -6 to 6
- expert_norm: float32 [2688], replicated, may hold values from 0.1 to 1.9
- router_weight: bfloat16 [2688, 16], replicated, may hold values from -0.125 to 0.125
- expert_index: int32 [2048, 6], P(('grp', 'seq', 'head')), may hold values from 0 to 15, all different within a row; in each aligned block of 64 rows (0 to 63, 64 to 127, ...) at most 32 rows name the same one
- up_weight: bfloat16 [32, 2688, 928], P(('seq', 'head')), may hold values from -0.125 to 0.125
- down_weight: bfloat16 [32, 928, 2688], P(('seq', 'head')), may hold values from -0.125 to 0.125
Outputs:
- layer_out: bfloat16 [2048, 2688], P(('grp', 'seq', 'head'))
Inputs may be any that keep to these rules, and one draw needn't show every extreme that they name: `expert_index`: each row names 6 different experts. In the rows of one device (aligned blocks of 64 rows) no expert is named more than 32 times, a bound that some block reaches.
All inputs are finite; a program needn't handle non-finite values.
Results may differ from a plain program's by a relative error of at most 0.019.
Values may be sent and summed in bfloat16 or wider, within the bound.
No kernel may reach another device: no remote copies, remote signals or barrier semaphores. Data moves between devices by JAX's collectives and lax.ppermute only.
A program may use at most 64 MiB of HBM per device.

v0:
```python
import jax
import jax.numpy as jnp
from jax import lax
from jax.sharding import PartitionSpec as P

HEADS = 64
HEAD_DIM = 64
STATE = 128
GROUPS = 8
TOP = 6
BLOCK_LEN = 256


EPSILON = 1e-05
ROUTE_SCALE = 2.5


def entering(x, axis, combine, identity):
    size, mine = (lax.axis_size(axis), lax.axis_index(axis))
    everything = jax.tree.map(
        lambda part, kind: lax.all_gather(part.astype(kind), axis), x, (jnp.bfloat16, jnp.bfloat16)
    )
    start = jax.tree.map(
        lambda part, zero: jnp.broadcast_to(jnp.asarray(zero, part.dtype), part.shape), x, identity
    )

    def turn(k, before):
        reached = k < mine
        new = combine(
            before, jax.tree.map(lambda part, own: part[k].astype(own.dtype), everything, x)
        )
        return jax.tree.map(lambda a, b: jnp.where(reached, a, b), new, before)

    return lax.fori_loop(0, size, turn, start)


def partner(x, axis, stride):
    return lax.ppermute(x, axis, [(i, i ^ 1 << stride) for i in range(lax.axis_size(axis))])


def expert_half(slot_rows, up_weight, down_weight):
    model_width = slot_rows.shape[-1]
    flat_rows = slot_rows.reshape(-1, model_width)
    activation = jnp.dot(flat_rows, up_weight[0], preferred_element_type=jnp.float32)
    activation = jnp.maximum(activation, 0.0)
    activation = (activation * activation).astype(jnp.bfloat16)
    output = jnp.dot(activation, down_weight[0], preferred_element_type=jnp.float32).astype(
        jnp.bfloat16
    )
    return output.reshape(slot_rows.shape)


def per_device(
    ssm_values,
    ssm_gate,
    write_proj,
    read_proj,
    step_size,
    decay_power,
    skip_gain,
    norm_gain,
    out_weight,
    residual,
    expert_norm,
    router_weight,
    expert_index,
    up_weight,
    down_weight,
):
    tokens_dev = ssm_values.shape[0]
    heads_dev = step_size.shape[1]
    per_group = HEADS // GROUPS
    groups_dev = heads_dev // per_group
    count_blocks = tokens_dev // BLOCK_LEN
    decay_rates = jnp.exp2(-decay_power.astype(jnp.float32))
    values = ssm_values.reshape(count_blocks, BLOCK_LEN, heads_dev, HEAD_DIM)
    steps_all = step_size.reshape(count_blocks, BLOCK_LEN, heads_dev)
    writes = write_proj.reshape(count_blocks, BLOCK_LEN, groups_dev, STATE)
    reads = read_proj.reshape(count_blocks, BLOCK_LEN, groups_dev, STATE)
    causal = jnp.tril(jnp.ones((BLOCK_LEN, BLOCK_LEN), dtype=bool))

    def one_block(pieces):
        values_in, steps_in, write_in, read_in = pieces
        log_decay = -steps_in * decay_rates[None, :]
        cumulative = jnp.cumsum(log_decay, axis=0)
        scores = jnp.einsum("tgn,sgn->gts", read_in, write_in, preferred_element_type=jnp.float32)
        scores = jnp.repeat(scores, per_group, axis=0)
        decays = jnp.exp(cumulative.T[:, :, None] - cumulative.T[:, None, :])
        mixing = jnp.where(causal[None], scores * decays * steps_in.T[:, None, :], 0.0).astype(
            jnp.bfloat16
        )
        inner_out = jnp.einsum(
            "hts,shp->thp", mixing, values_in, preferred_element_type=jnp.float32
        )
        block_total = cumulative[-1]
        weighted = (
            values_in.astype(jnp.float32)
            * (jnp.exp(block_total[None, :] - cumulative) * steps_in)[:, :, None]
        ).astype(jnp.bfloat16)
        write_heads = jnp.repeat(write_in, per_group, axis=1)
        fresh_state = jnp.einsum(
            "shp,shn->hpn", weighted, write_heads, preferred_element_type=jnp.float32
        )
        return (inner_out, fresh_state, block_total, cumulative)

    inner_all, fresh_all, totals_blk, cumul_all = lax.map(
        one_block, (values, steps_all, writes, reads)
    )

    def summarize(carried_in, pieces):
        decay_prod, summary = carried_in
        block_total, fresh_state = pieces
        factor = jnp.exp(block_total)
        return ((decay_prod * factor, factor[:, None, None] * summary + fresh_state), None)

    zero_state = jnp.zeros((heads_dev, HEAD_DIM, STATE), jnp.float32)
    (device_decay, device_state), unused = lax.scan(
        summarize, (jnp.ones((heads_dev,), jnp.float32), zero_state), (totals_blk, fresh_all)
    )

    def combine(earlier, later):
        return (earlier[0] * later[0], later[0][:, None, None] * earlier[1] + later[1])

    identity = (jnp.ones_like(device_decay), jnp.zeros_like(device_state))
    prior_decay, incoming = entering((device_decay, device_state), "seq", combine, identity)

    def emit_rows(carry_state, pieces):
        read_in, cumulative, block_total, fresh_state = pieces
        read_heads = jnp.repeat(read_in, per_group, axis=1)
        carried = jnp.einsum(
            "thn,hpn->thp",
            read_heads,
            carry_state.astype(jnp.bfloat16),
            preferred_element_type=jnp.float32,
        )
        carried = carried * jnp.exp(cumulative)[:, :, None]
        return (jnp.exp(block_total)[:, None, None] * carry_state + fresh_state, carried)

    final_state, carried_all = lax.scan(
        emit_rows, incoming, (reads, cumul_all, totals_blk, fresh_all)
    )
    values_flat = ssm_values.reshape(tokens_dev, heads_dev, HEAD_DIM).astype(jnp.float32)
    ssm_out = (inner_all + carried_all).reshape(tokens_dev, heads_dev, HEAD_DIM) + skip_gain[
        None, :, None
    ] * values_flat
    gate_vals = ssm_gate.reshape(tokens_dev, heads_dev, HEAD_DIM).astype(jnp.float32)
    gated = (ssm_out * jax.nn.silu(gate_vals)).reshape(tokens_dev, groups_dev, per_group * HEAD_DIM)
    inv_rms = lax.rsqrt(jnp.mean(gated * gated, axis=-1, keepdims=True) + EPSILON)
    normed = (
        (gated * inv_rms).reshape(tokens_dev, heads_dev * HEAD_DIM) * norm_gain[None, :]
    ).astype(jnp.bfloat16)
    weight_full = lax.all_gather(out_weight, "seq", axis=1, tiled=True)
    rows_own = tokens_dev // lax.axis_size("head")
    mixed_out = lax.psum_scatter(
        jnp.dot(normed, weight_full, preferred_element_type=jnp.float32).astype(jnp.bfloat16),
        "head",
        scatter_dimension=0,
        tiled=True,
    ).astype(jnp.float32)
    hidden = residual.astype(jnp.float32) + mixed_out
    inputs = (
        hidden
        * lax.rsqrt(jnp.mean(hidden * hidden, axis=-1, keepdims=True) + EPSILON)
        * expert_norm[None, :]
    ).astype(jnp.bfloat16)
    logits = jnp.dot(inputs, router_weight, preferred_element_type=jnp.float32)
    experts = router_weight.shape[1]
    model_width = inputs.shape[1]
    expert_hits = expert_index[:, :, None] == jnp.arange(experts, dtype=jnp.int32)[None, None, :]
    picked = jnp.sum(jnp.where(expert_hits, logits[:, None, :], 0.0), axis=-1)
    probability = jax.nn.sigmoid(picked)
    shares = ROUTE_SCALE * probability / jnp.sum(probability, axis=1, keepdims=True)
    capacity = (
        8
        * TOP
        * tokens_dev
        // (3 * lax.axis_size("seq") * lax.axis_size("head") * lax.axis_size("head"))
    )
    flat_hits = expert_hits.astype(jnp.int32).reshape(rows_own * TOP, experts)
    before = jnp.cumsum(flat_hits, axis=0) - flat_hits
    slot_index = jnp.sum(before * flat_hits, axis=1)
    target = expert_index.reshape(rows_own * TOP) * capacity + slot_index
    placing = jnp.arange(experts * capacity, dtype=jnp.int32)[:, None] == target[None, :]
    placing = jnp.any(placing.reshape(experts * capacity, rows_own, TOP), axis=2).astype(
        jnp.bfloat16
    )
    outgoing = jnp.dot(placing, inputs, preferred_element_type=jnp.float32).astype(jnp.bfloat16)
    outgoing = outgoing.reshape(experts, capacity, model_width)
    halves = outgoing.reshape(experts, 2, capacity // 2, model_width).reshape(
        2 * experts, capacity // 2, model_width
    )
    slot_rows = lax.all_to_all(halves, ("seq", "head"), split_axis=0, concat_axis=0, tiled=True)
    other_rows = partner(slot_rows, "head", 0)
    both_rows = jnp.concatenate([slot_rows, other_rows], axis=1)
    both_parts = expert_half(both_rows, up_weight, down_weight)
    own_part = both_parts[:, : slot_rows.shape[1]]
    other_part = both_parts[:, slot_rows.shape[1] :]
    back_part = partner(other_part, "head", 0)
    summed = (own_part.astype(jnp.float32) + back_part.astype(jnp.float32)).astype(jnp.bfloat16)
    returned = lax.all_to_all(summed, ("seq", "head"), split_axis=0, concat_axis=0, tiled=True)
    results = returned.reshape(experts, 2, capacity // 2, model_width).reshape(
        experts, capacity, model_width
    )
    gathered = results.reshape(experts * capacity, model_width)[target].reshape(
        rows_own, TOP, model_width
    )
    moe_out = jnp.sum(shares[:, :, None] * gathered.astype(jnp.float32), axis=1)
    return (hidden + moe_out).astype(jnp.bfloat16)


def solution(mesh):
    return jax.shard_map(
        per_device,
        mesh=mesh,
        in_specs=(
            P(("grp", "seq"), "head"),
            P(("grp", "seq"), "head"),
            P(("grp", "seq"), "head"),
            P(("grp", "seq"), "head"),
            P(("grp", "seq"), "head"),
            P("head"),
            P("head"),
            P("head"),
            P("head", "seq"),
            P(("grp", "seq", "head"), None),
            P(),
            P(),
            P(("grp", "seq", "head"), None),
            P(("seq", "head"), None, None),
            P(("seq", "head"), None, None),
        ),
        out_specs=P(("grp", "seq", "head"), None),
        check_vma=False,
    )
```

profile of v0, /device:TPU:0, one launch (start us, length us, event | category | flops | bytes accessed | tf_op | source)
XLA Modules:
  0.0 378.8 jit_solution(6927901179226233715)
XLA Ops:
  6.6 0.7 multiply_exponential_fusion
  7.3 0.8 copy_bitcast_fusion.3
  8.1 0.6 reduce-window.14
  9.1 0.8 exponential_multiply_fusion
  10.0 1.2 copy.62
  11.3 0.2 broadcast_in_dim.95
  11.5 1.0 fusion.11
  12.5 0.7 all-gather.5.cloned.1.call-update
  13.5 22.3 %all-gather.1 = bf16[8,1,16]{2,1,0:T(2,128)(2,1)S(1)} all-gather(bf16[1,1,16]{2,1,0:T(2,128)(2,1)S(1)} %bitcast.150), channel_id=1, replica_groups=mesh['grp'=1,'seq'=8,'head'=4] {'seq'}, dimensions={0}, use_global_device_ids=true | all-gather | bytes 288 | tf_op jit(solution)/shard_map/all_gather | solution.py:21
  35.8 0.2 copy.66
  36.3 0.2 fusion.35
  36.5 1.2 fusion.6
  37.7 0.8 convolution_bitcast_fusion
  38.5 26.0 %all-gather.7.cloned.1.call-done = bf16[128,64,128]{2,1,0:T(8,128)(2,1)} async-done(((bf16[16,64,128]{2,1,0:T(8,128)(2,1)}), bf16[128,64,128]{2,1,0:T(8,128)(2,1)}) %all-gather.7.cloned.1.call-update) | async-done | bytes 2097168 | tf_op jit(solution)/shard_map/all_gather | solution.py:21
  64.5 9.1 %while.9 = (s32[]{:T(128)}, f32[16,64,128]{2,1,0:T(8,128)S(1)}, s32[]{:T(128)}, bf16[8,16]{1,0:T(8,128)(2,1)S(1)}, bf16[8,16,64,128]{3,2,1,0:T(8,128)(2,1)}, /*index=5*/s32[]{:T(128)}, s32[]{:T(128)}) while((s32[]{:T(128)}, f32[16,64,128]{2,1,0:T(8,128)S(1)}, s32[]{:T(128)}, bf16[8,16]{1,0:T(8,128)(2,1)S(1)}, ...), condition=%wide.region_3.4_spmd.clone, body=%wide.region_2.3_spmd.clone.sunk | while | flops 655380 | bytes 1310985 | solution.py:34
  64.5 1.1 fusion.61
  65.7 1.1 fusion.61
  66.8 1.1 fusion.61
  67.9 1.1 fusion.61
  69.0 1.1 fusion.61
  70.2 1.1 fusion.61
  71.3 1.1 fusion.61
  72.5 1.1 fusion.61
  73.8 1.7 fusion.16
  75.7 0.3 mul.253
  76.0 0.2 copy.80
  76.2 1.6 copy.65
  77.8 76.6 %all-gather.5.cloned.1.call-done = bf16[1024,2688]{0,1:T(8,128)(2,1)} async-done(((bf16[1024,336]{0,1:T(8,128)(2,1)}), bf16[1024,2688]{0,1:T(8,128)(2,1)}) %all-gather.5.cloned.1.call-update) | async-done | bytes 5505040 | tf_op jit(solution)/shard_map/all_gather | solution.py:152
  154.4 5.9 %convolution_convert_fusion.2 = bf16[256,2688]{1,0:T(8,128)(2,1)} fusion(bf16[1024,2688]{0,1:T(8,128)(2,1)} %all-gather.5.cloned.1.call-done, f32[256,1024]{1,0:T(8,128)S(1)} %bitcast.145, f32[256,1024]{1,0:T(8,128)S(1)} %copy.65, bf16[256,1024]{1,0:T(8,128)(2,1)} %param.17, f32[1024]{0:T(1024)S(1)} %copy-done.13, f32[1024]{0:T(1024)S(1)} %mul.243, ...), kind=kOutput, calls=%fused_computation.16 | convolution fusion | flops 1413120000 | bytes 10035200 | tf_op jit(solution)/shard_map/dot_general | solution.py:155
  160.7 0.9 reduce-window.16
  161.6 0.2 slice_reduce_fusion
  162.4 23.1 %reduce-scatter.2.cloned.1.call-done = bf16[64,2688]{1,0:T(8,128)(2,1)} async-done(((bf16[256,2688]{1,0:T(8,128)(2,1)}), bf16[64,2688]{1,0:T(8,128)(2,1)}) %reduce-scatter.2.cloned.1.call-update) | async-done | bytes 344080 | tf_op jit(solution)/shard_map/reduce_scatter | solution.py:154
  185.5 1.2 multiply_reduce_fusion.1
  186.7 1.1 multiply_convert_fusion.2
  187.8 0.9 convolution_convert_fusion.1
  188.7 67.3 %all_to_all.10 = bf16[32,16,2688]{2,1,0:T(8,128)(2,1)S(1)} all-to-all(bf16[32,16,2688]{2,1,0:T(8,128)(2,1)S(1)} %bitcast.138), channel_id=1, replica_groups=mesh['grp'=1,'seq'=8,'head'=4] {'seq','head'}, dimensions={0} | all-to-all | bytes 5505024 | tf_op jit(solution)/shard_map/all_to_all | solution.py:192
  256.2 5.0 %collective-permute-done = bf16[32,16,2688]{2,1,0:T(8,128)(2,1)S(1)} collective-permute-done((bf16[32,16,2688]{2,1,0:T(8,128)(2,1)S(1)}, bf16[32,16,2688]{2,1,0:T(8,128)(2,1)S(1)}, u32[]{:S(2)}, u32[]{:S(2)}) %collective-permute-start) | collective-permute-done | bytes 2752544 | tf_op jit(solution)/shard_map/ppermute | solution.py:38
  261.2 2.8 pad_maximum_fusion
  264.0 18.9 %convolution_convert_fusion = bf16[1024,2688]{1,0:T(8,128)(2,1)} fusion(bf16[1,928,2688]{2,1,0:T(8,128)(2,1)} %param.31, bf16[1024,2688]{1,0:T(8,128)(2,1)} %bitcast.137, bf16[1,2688,928]{1,2,0:T(8,128)(2,1)} %param.30), kind=kOutput, calls=%fused_computation.4 | convolution fusion | flops 10222927872 | bytes 20987904 | tf_op jit(solution)/shard_map/dot_general | solution.py:47
  282.9 2.1 slice.35
  285.3 5.0 %collective-permute-done.1 = bf16[32,16,2688]{2,1,0:T(8,128)(2,1)S(1)} collective-permute-done((bf16[32,16,2688]{2,1,0:T(8,128)(2,1)S(1)}, bf16[32,16,2688]{2,1,0:T(8,128)(2,1)S(1)}, u32[]{:S(2)}, u32[]{:S(2)}) %collective-permute-start.1) | collective-permute-done | bytes 2752544 | tf_op jit(solution)/shard_map/ppermute | solution.py:38
  290.2 2.2 add_convert_fusion
  292.5 3.5 all-to-all-start.1
  296.5 62.3 %all-to-all-done.1 = bf16[32,16,2688]{2,1,0:T(8,128)(2,1)S(1)} async-done(((bf16[32,16,2688]{2,1,0:T(8,128)(2,1)}), bf16[32,16,2688]{2,1,0:T(8,128)(2,1)S(1)}, u32[]{:S(2)}, u32[]{:S(2)}) %all-to-all-start.1) | async-done | bytes 2752544 | tf_op jit(solution)/shard_map/all_to_all | solution.py:200
  358.8 3.4 gather_fusion
  362.2 4.6 %reshape.258 = f32[64,6,2688]{2,1,0:T(8,128)} reshape(bf16[384,2688]{1,0:T(8,128)(2,1)} %gather_fusion) | data formatting | bytes 6193152 | tf_op jit(solution)/shard_map/convert_element_type | solution.py:207
  366.8 4.6 %multiply_reduce_fusion = f32[64,2688]{1,0:T(8,128)S(1)} fusion(f32[64,6,2688]{2,1,0:T(8,128)} %reshape.258, f32[64,6]{1,0:T(8,128)S(1)} %copy.68), kind=kLoop, calls=%fused_computation.6 | loop fusion | flops 1892352 | bytes 4818432 | tf_op jit(solution)/shard_map/reduce_sum | solution.py:207
  371.4 0.8 add_convert_fusion.1
  (83 shorter events, 3.3 us)
Async XLA Ops:
  6.5 4.7 %copy-start = (bf16[256,256]{1,0:T(8,128)(2,1)S(1)}, bf16[256,256]{1,0:T(8,128)(2,1)}, u32[]{:S(2)}) copy-start(bf16[256,256]{1,0:T(8,128)(2,1)} %param.19) | copy-start | bytes 393220
  6.5 30.0 %copy-start.9 = (f32[256,16]{0,1:T(8,128)S(1)}, f32[256,16]{0,1:T(8,128)}, u32[]{:S(2)}) copy-start(f32[256,16]{0,1:T(8,128)} %param.21) | copy-start | bytes 49156
  6.5 29.3 %copy-start.6 = (bf16[256,1024]{1,0:T(8,128)(2,1)S(1)}, bf16[256,1024]{1,0:T(8,128)(2,1)}, u32[]{:S(2)}) copy-start(bf16[256,1024]{1,0:T(8,128)(2,1)} %param.18) | copy-start | bytes 1572868
  6.5 29.5 %copy-start.14 = (f32[16]{0:T(128)S(1)}, f32[16]{0:T(128)}, u32[]{:S(2)}) copy-start(f32[16]{0:T(128)} %param.23) | copy-start | bytes 196
  6.5 29.7 %copy-start.8 = (bf16[256,256]{1,0:T(8,128)(2,1)S(1)}, bf16[256,256]{1,0:T(8,128)(2,1)}, u32[]{:S(2)}) copy-start(bf16[256,256]{1,0:T(8,128)(2,1)} %param.20) | copy-start | bytes 393220
  6.5 58.0 %all-gather.7.cloned.1.call-start = ((), (), s32[]{:S(2)}) async-start(), calls=%async_computation.5 | async-start | bytes 2359296 | tf_op jit(solution)/shard_map/all_gather | solution.py:21
  12.5 141.9 %all-gather.5.cloned.1.call-start = ((), (), s32[]{:S(2)}) async-start(), calls=%async_computation.3 | async-start | bytes 6193152 | tf_op jit(solution)/shard_map/all_gather | solution.py:152
  13.3 172.2 %reduce-scatter.2.cloned.1.call-start = ((), (), s32[]{:S(2)}) async-start(), calls=%async_computation.4 | async-start | bytes 1720320 | tf_op jit(solution)/shard_map/reduce_scatter | solution.py:154
  75.5 78.9 %copy-start.7 = (bf16[256,1024]{1,0:T(8,128)(2,1)S(1)}, bf16[256,1024]{1,0:T(8,128)(2,1)}, u32[]{:S(2)}) copy-start(bf16[256,1024]{1,0:T(8,128)(2,1)} %param.18) | copy-start | bytes 1572868
  75.5 78.9 %copy-start.13 = (f32[1024]{0:T(1024)S(1)}, f32[1024]{0:T(1024)}, u32[]{:S(2)}) copy-start(f32[1024]{0:T(1024)} %param.24) | copy-start | bytes 12292
  154.4 6.0 %copy-start.11 = (s32[64,6]{0,1:T(8,128)S(1)}, s32[64,6]{0,1:T(8,128)}, u32[]{:S(2)}) copy-start(s32[64,6]{0,1:T(8,128)} %param.29) | copy-start | bytes 4612
  154.4 31.1 %copy-start.3 = (bf16[64,2688]{1,0:T(8,128)(2,1)S(1)}, bf16[64,2688]{1,0:T(8,128)(2,1)}, u32[]{:S(2)}) copy-start(bf16[64,2688]{1,0:T(8,128)(2,1)} %param.26) | copy-start | bytes 1032196
  154.4 32.3 %copy-start.12 = (f32[2688]{0:T(1024)S(1)}, f32[2688]{0:T(1024)}, u32[]{:S(2)}) copy-start(f32[2688]{0:T(1024)} %param.27) | copy-start | bytes 32260
  256.1 5.1 %collective-permute-start = (bf16[32,16,2688]{2,1,0:T(8,128)(2,1)S(1)}, bf16[32,16,2688]{2,1,0:T(8,128)(2,1)S(1)}, u32[]{:S(2)}, u32[]{:S(2)}) collective-permute-start(bf16[32,16,2688]{2,1,0:T(8,128)(2,1)S(1)} %all_to_all.10), channel_id=1, source_target_pairs={{0,1},{1,0},{2,3},{3,2},{4,5},{5,4},{6,7},{7,6},{8,9},{9,8},{10,11... | collective-permute-start | bytes 8257544 | tf_op jit(solution)/shard_map/ppermute | solution.py:38
  282.9 7.3 %copy-start.2 = (bf16[1024,2688]{1,0:T(8,128)(2,1)S(1)}, bf16[1024,2688]{1,0:T(8,128)(2,1)}, u32[]{:S(2)}) copy-start(bf16[1024,2688]{1,0:T(8,128)(2,1)} %convolution_convert_fusion) | copy-start | bytes 16515076
  285.1 5.2 %collective-permute-start.1 = (bf16[32,16,2688]{2,1,0:T(8,128)(2,1)S(1)}, bf16[32,16,2688]{2,1,0:T(8,128)(2,1)S(1)}, u32[]{:S(2)}, u32[]{:S(2)}) collective-permute-start(bf16[32,16,2688]{2,1,0:T(8,128)(2,1)S(1)} %slice.35), channel_id=1, source_target_pairs={{0,1},{1,0},{2,3},{3,2},{4,5},{5,4},{6,7},{7,6},{8,9},{9,8},{10,11... | collective-permute-start | bytes 8257544 | tf_op jit(solution)/shard_map/ppermute | solution.py:38
  292.5 3.6 copy-start.10
  292.5 66.4 %all-to-all-start.1 = ((bf16[32,16,2688]{2,1,0:T(8,128)(2,1)}), bf16[32,16,2688]{2,1,0:T(8,128)(2,1)S(1)}, u32[]{:S(2)}, u32[]{:S(2)}) async-start(bf16[32,16,2688]{2,1,0:T(8,128)(2,1)} %add_convert_fusion), calls=%async_computation.2 | async-start | bytes 5505024 | tf_op jit(solution)/shard_map/all_to_all | solution.py:200
  362.2 10.0 %copy-start.1 = (bf16[256,256]{1,0:T(8,128)(2,1)S(1)}, bf16[256,256]{1,0:T(8,128)(2,1)}, u32[]{:S(2)}) copy-start(bf16[256,256]{1,0:T(8,128)(2,1)} %param.19) | copy-start | bytes 393220
  366.8 4.6 %copy-start.4 = (bf16[64,2688]{1,0:T(8,128)(2,1)S(1)}, bf16[64,2688]{1,0:T(8,128)(2,1)}, u32[]{:S(2)}) copy-start(bf16[64,2688]{1,0:T(8,128)(2,1)} %param.26) | copy-start | bytes 1032196
  366.8 4.6 %copy-start.5 = (bf16[64,2688]{1,0:T(8,128)(2,1)S(1)}, bf16[64,2688]{1,0:T(8,128)(2,1)}, u32[]{:S(2)}) copy-start(bf16[64,2688]{1,0:T(8,128)(2,1)} %reduce-scatter.2.cloned.1.call-done) | copy-start | bytes 1032196
Sparse Core Ops, SparseCore 0:
  12.6 51.8 all-gather.6
  66.7 87.6 all-gather.4
  160.5 24.9 reduce-scatter.1
where the time goes:
time: 380 us; the launch traced here: 379 us
  waiting for transfers between devices  199 us (52%)
  blocking collectives  89.6 us (24%)
  matrix products  29.6 us (8%)
  other arithmetic  27.3 us (7%)
  local copies, waits for them, and re-layouts  15.9 us (4%)
  between operations  13.5 us (4%)
  starting transfers between devices  3.85 us (1%)
    all_gather x1, waiting for transfers between devices, per_device(): weight_full = lax.all_gather(out_weight, 'seq', axis=1, tiled=True)  76.6 us
    all_to_all x1, blocking collectives, per_device(): lax.all_to_all(halves, ('seq', 'head'), split_axis=0, concat_axis=0, tile...  67.3 us
    all_to_all x1, waiting for transfers between devices, per_device(): lax.all_to_all(summed, ('seq', 'head'), split_axis=0, concat_axis=0, tile...  62.3 us
    all_gather x1, waiting for transfers between devices, entering(): lax.all_gather(part.astype(kind), axis)  26 us
    reduce_scatter x1, waiting for transfers between devices, per_device(): lax.psum_scatter(jnp.dot(normed, weight_full, preferred_element_type=jnp....  23.1 us
    all_gather x1, blocking collectives, entering(): lax.all_gather(part.astype(kind), axis)  22.3 us
    dot_general x1, matrix products, expert_half(): jnp.dot(activation, down_weight[0], preferred_element_type=jnp.float32)  18.9 us
    ppermute x2, waiting for transfers between devices, partner(): lax.ppermute(x, axis, [(i, i ^ 1 << stride) for i in range(lax.axis_size(...  9.99 us
  transfers between devices with their start and end apart: 6, of which 6 were waited for; matrix products, arithmetic and copies ran while one was open for 5% of the time, Pallas kernels for 0%

commit v1 on v0

--- a/solution.py
+++ b/solution.py
@@ -15,23 +15,108 @@
 ROUTE_SCALE = 2.5
 
 
-def entering(x, axis, combine, identity):
-    size, mine = (lax.axis_size(axis), lax.axis_index(axis))
-    everything = jax.tree.map(
-        lambda part, kind: lax.all_gather(part.astype(kind), axis), x, (jnp.bfloat16, jnp.bfloat16)
-    )
-    start = jax.tree.map(
-        lambda part, zero: jnp.broadcast_to(jnp.asarray(zero, part.dtype), part.shape), x, identity
-    )
-
-    def turn(k, before):
-        reached = k < mine
-        new = combine(
-            before, jax.tree.map(lambda part, own: part[k].astype(own.dtype), everything, x)
-        )
-        return jax.tree.map(lambda a, b: jnp.where(reached, a, b), new, before)
-
-    return lax.fori_loop(0, size, turn, start)
+def seq_ring(size):
+    return list(range(0, size, 2)) + list(range(1, size, 2))[::-1]
+
+
+def shift(x, axis, order, step):
+    size = len(order)
+    return lax.ppermute(x, axis, [(order[i], order[(i + step) % size]) for i in range(size)])
+
+
+def pick(parts, index):
+    return lax.dynamic_index_in_dim(parts, index, 0, keepdims=False)
+
+
+def packed(state, decay):
+    high = decay.astype(jnp.bfloat16)
+    low = (decay - high.astype(jnp.float32)).astype(jnp.bfloat16)
+    rows = jnp.zeros((16, STATE), jnp.bfloat16)
+    rows = rows.at[0, : decay.shape[0]].set(high).at[1, : decay.shape[0]].set(low)
+    return jnp.concatenate([state.reshape(-1, STATE).astype(jnp.bfloat16), rows], axis=0)
+
+
+def unpacked(block, heads):
+    rows = heads * HEAD_DIM
+    state = block[:rows].astype(jnp.float32).reshape(heads, HEAD_DIM, STATE)
+    decay = block[rows, :heads].astype(jnp.float32) + block[rows + 1, :heads].astype(jnp.float32)
+    return state, decay
+
+
+def entering(decay, state, axis):
+    size, mine = lax.axis_size(axis), lax.axis_index(axis)
+    half = decay.shape[0] // 2
+    odd = mine % 2 == 1
+    swap = [(i, i ^ 1) for i in range(size)]
+    states = state.reshape(2, half, HEAD_DIM, STATE)
+    decays = decay.reshape(2, half)
+    side = mine % 2
+    got = lax.ppermute(packed(pick(states, 1 - side), pick(decays, 1 - side)), axis, swap)
+    other_state, other_decay = unpacked(got, half)
+    own_state, own_decay = pick(states, side), pick(decays, side)
+    first_state = jnp.where(odd, other_state, own_state)
+    second_state = jnp.where(odd, own_state, other_state)
+    first_decay = jnp.where(odd, other_decay, own_decay)
+    second_decay = jnp.where(odd, own_decay, other_decay)
+    pair = packed(
+        second_decay[:, None, None] * first_state + second_state, first_decay * second_decay
+    )
+    before = None
+    received = [
+        lax.ppermute(pair, axis, [(i, i + 2 * d) for i in range(size - 2 * d)])
+        for d in range(1, size // 2)
+    ]
+    for block in received[::-1]:
+        block_state, block_decay = unpacked(block, half)
+        before = (
+            block_state
+            if before is None
+            else block_decay[:, None, None] * before + block_state
+        )
+    if before is None:
+        before = jnp.zeros_like(first_state)
+    inner = first_decay[:, None, None] * before + first_state
+    mine_half = jnp.where(odd, inner, before)
+    send_half = jnp.where(odd, before, inner).astype(jnp.bfloat16)
+    back = lax.ppermute(send_half.reshape(-1, STATE), axis, swap)
+    back = back.astype(jnp.float32).reshape(mine_half.shape)
+    low = jnp.where(odd, back, mine_half)
+    high = jnp.where(odd, mine_half, back)
+    return jnp.concatenate([low, high], axis=0)
+
+
+def ring_weights(out_weight, axis):
+    size = lax.axis_size(axis)
+    order = seq_ring(size)
+    shard = out_weight.T
+    cut = (shard.shape[0] // 2 + 15) // 16 * 16
+    top, bottom = shard[:cut], shard[cut:]
+    groups = [([0], [shard])]
+    ahead, behind = (top, bottom), (top, bottom)
+    for step in range(1, size // 2 + 1):
+        if 2 * step < size:
+            ahead = tuple(shift(part, axis, order, 1) for part in ahead)
+            behind = tuple(shift(part, axis, order, -1) for part in behind)
+            groups.append(([-step, step], [*ahead, *behind]))
+        else:
+            last = (shift(ahead[0], axis, order, 1), shift(behind[1], axis, order, -1))
+            groups.append(([-step], [*last]))
+    return groups
+
+
+def head_scatter(pieces, axis):
+    size, mine = lax.axis_size(axis), lax.axis_index(axis)
+    stride = 1
+    while stride < size:
+        bit = (mine // stride) % 2
+        left = pieces.shape[0] // 2
+        view = pieces.reshape(left, 2, *pieces.shape[1:])
+        send = lax.dynamic_index_in_dim(view, 1 - bit, 1, keepdims=False)
+        keep = lax.dynamic_index_in_dim(view, bit, 1, keepdims=False)
+        came = lax.ppermute(send, axis, [(i, i ^ stride) for i in range(size)])
+        pieces = (keep.astype(jnp.float32) + came.astype(jnp.float32)).astype(jnp.bfloat16)
+        stride *= 2
+    return pieces[0]
 
 
 def partner(x, axis, stride):
@@ -72,6 +157,7 @@
     per_group = HEADS // GROUPS
     groups_dev = heads_dev // per_group
     count_blocks = tokens_dev // BLOCK_LEN
+    weight_groups = ring_weights(out_weight, "seq")
     decay_rates = jnp.exp2(-decay_power.astype(jnp.float32))
     values = ssm_values.reshape(count_blocks, BLOCK_LEN, heads_dev, HEAD_DIM)
     steps_all = step_size.reshape(count_blocks, BLOCK_LEN, heads_dev)
@@ -118,11 +204,7 @@
         summarize, (jnp.ones((heads_dev,), jnp.float32), zero_state), (totals_blk, fresh_all)
     )
 
-    def combine(earlier, later):
-        return (earlier[0] * later[0], later[0][:, None, None] * earlier[1] + later[1])
-
-    identity = (jnp.ones_like(device_decay), jnp.zeros_like(device_state))
-    prior_decay, incoming = entering((device_decay, device_state), "seq", combine, identity)
+    incoming = entering(device_decay, device_state, "seq")
 
     def emit_rows(carry_state, pieces):
         read_in, cumulative, block_total, fresh_state = pieces
@@ -149,14 +231,32 @@
     normed = (
         (gated * inv_rms).reshape(tokens_dev, heads_dev * HEAD_DIM) * norm_gain[None, :]
     ).astype(jnp.bfloat16)
-    weight_full = lax.all_gather(out_weight, "seq", axis=1, tiled=True)
-    rows_own = tokens_dev // lax.axis_size("head")
-    mixed_out = lax.psum_scatter(
-        jnp.dot(normed, weight_full, preferred_element_type=jnp.float32).astype(jnp.bfloat16),
-        "head",
-        scatter_dimension=0,
-        tiled=True,
-    ).astype(jnp.float32)
+    seq_size = lax.axis_size("seq")
+    head_size = lax.axis_size("head")
+    rows_own = tokens_dev // head_size
+    shard_width = out_weight.shape[1]
+    offsets, products = [], []
+    for steps, parts in weight_groups:
+        rows = parts[0] if len(parts) == 1 else jnp.concatenate(parts, axis=0)
+        product = lax.dot_general(
+            normed, rows, (((1,), (1,)), ((), ())), preferred_element_type=jnp.float32
+        ).astype(jnp.bfloat16)
+        for at, step in enumerate(steps):
+            offsets.append(step)
+            products.append(product[:, at * shard_width : (at + 1) * shard_width])
+    stacked = jnp.stack(products, axis=0).reshape(
+        seq_size, head_size, rows_own, shard_width
+    )
+    scattered = head_scatter(stacked.transpose(1, 0, 2, 3), "head").astype(jnp.float32)
+    order = seq_ring(seq_size)
+    table = [[0] * seq_size for _ in range(seq_size)]
+    for place, index in enumerate(order):
+        for at, step in enumerate(offsets):
+            table[index][order[(place + step) % seq_size]] = at
+    places = jnp.asarray(table, jnp.int32)[lax.axis_index("seq")]
+    mixed_out = jnp.concatenate(
+        [pick(scattered, places[b]) for b in range(seq_size)], axis=1
+    )
     hidden = residual.astype(jnp.float32) + mixed_out
     inputs = (
         hidden

time: 380 us -> 308 us (0.81)
  waiting for transfers between devices: 199 us -> 100 us
  starting transfers between devices: 3.85 us -> 40.4 us
  blocking collectives: 89.6 us -> 68.2 us
  local copies, waits for them, and re-layouts: 15.9 us -> 28.2 us
  other arithmetic: 27.3 us -> 23.5 us
    all_gather x2 -> x0, waiting for transfers between devices: 103 us -> none  [the longest x1 76.6 us: per_device(): weight_full = lax.all_gather(out_weight, 'seq', axis=1, tiled=True)]
    ppermute x0 -> x21, starting transfers between devices: none -> 36.5 us  [the longest x14 16 us: shift(): lax.ppermute(x, axis, [(order[i], order[(i + step) % size]) for i in rang...]
    ppermute x0 -> x21, waiting for transfers between devices: none -> 28.2 us  [the longest x14 15.4 us: shift(): lax.ppermute(x, axis, [(order[i], order[(i + step) % size]) for i in rang...]
    reduce_scatter x1 -> x0, waiting for transfers between devices: 23.1 us -> none  [per_device(): lax.psum_scatter(jnp.dot(normed, weight_full, preferred_element_type=jnp....]
    all_gather x1 -> x0, blocking collectives: 22.3 us -> none  [entering(): lax.all_gather(part.astype(kind), axis)]
    select_n x8 -> x0, other arithmetic: 8.78 us -> none  [turn(): return jax.tree.map(lambda a, b: jnp.where(reached, a, b), new, before)]
    slice x0 -> x12, local copies, waits for them, and re-layouts: none -> 5.22 us  [the longest x2 3.5 us: ring_weights(): top, bottom = (shard[:cut], shard[cut:])]
    convert_element_type x9 -> x12, other arithmetic: 0.24 us -> 4.2 us  [the longest x4 1.89 us: unpacked(): state = block[:rows].astype(jnp.float32).reshape(heads, HEAD_DIM, STATE)]
  transfers between devices with their start and end apart: 6 -> 24, of which waited for: 6 -> 14; matrix products, arithmetic and copies ran while one was open for 5% -> 12% of each run, Pallas kernels for 0% -> 0%
where the time goes in v1:
time: 308 us; the launch traced here: 307 us
  waiting for transfers between devices  100 us (32%)
  blocking collectives  68.2 us (22%)
  starting transfers between devices  40.4 us (13%)
  matrix products  30.3 us (10%)
  local copies, waits for them, and re-layouts  28.2 us (9%)
  other arithmetic  23.5 us (8%)
  between operations  15.8 us (5%)
    all_to_all x1, blocking collectives, per_device(): lax.all_to_all(halves, ('seq', 'head'), split_axis=0, concat_axis=0, tile...  68.2 us
    all_to_all x1, waiting for transfers between devices, per_device(): lax.all_to_all(summed, ('seq', 'head'), split_axis=0, concat_axis=0, tile...  62.2 us
    dot_general x1, matrix products, expert_half(): jnp.dot(activation, down_weight[0], preferred_element_type=jnp.float32)  18.9 us
    ppermute x14, starting transfers between devices, shift(): lax.ppermute(x, axis, [(order[i], order[(i + step) % size]) for i in rang...  16 us
    ppermute x3, starting transfers between devices, entering(): lax.ppermute(pair, axis, [(i, i + 2 * d) for i in range(size - 2 * d)])  15.9 us
    ppermute x14, waiting for transfers between devices, shift(): lax.ppermute(x, axis, [(order[i], order[(i + step) % size]) for i in rang...  15.4 us
    ppermute x2, waiting for transfers between devices, partner(): lax.ppermute(x, axis, [(i, i ^ 1 << stride) for i in range(lax.axis_size(...  9.99 us
    dot_general x5, matrix products, per_device(): lax.dot_general(normed, rows, (((1,), (1,)), ((), ())), preferred_element...  7.28 us
  transfers between devices with their start and end apart: 24, of which 14 were waited for; matrix products, arithmetic and copies ran while one was open for 12% of the time, Pallas kernels for 0%

profile of v1, /device:TPU:0, one launch (start us, length us, event | category | flops | bytes accessed | tf_op | source)
XLA Modules:
  0.0 306.8 jit_solution(10852218941891340169)
XLA Ops:
  0.0 1.8 slice.224
  1.8 3.0 collective-permute-start.8
  4.8 1.8 slice.223
  6.6 2.0 collective-permute-start.7
  11.2 1.4 exponential_multiply_fusion
  12.6 1.3 copy.81
  14.8 2.0 collective-permute-start
  17.1 1.2 fusion.5
  19.4 1.2 copy.85
  20.6 4.2 %collective-permute-done = bf16[528,128]{1,0:T(8,128)(2,1)S(1)} collective-permute-done((bf16[528,128]{1,0:T(8,128)(2,1)S(1)}, bf16[528,128]{1,0:T(8,128)(2,1)S(1)}, u32[]{:S(2)}, u32[]{:S(2)}) %collective-permute-start) | collective-permute-done | bytes 135200 | tf_op jit(solution)/shard_map/ppermute | solution.py:54
  26.6 1.3 collective-permute-start.2
  27.9 2.8 collective-permute-done.2
  30.7 6.9 %collective-permute-start.1 = (bf16[528,128]{1,0:T(8,128)(2,1)}, bf16[528,128]{1,0:T(8,128)(2,1)}, u32[]{:S(2)}, u32[]{:S(2)}) collective-permute-start(bf16[528,128]{1,0:T(8,128)(2,1)} %pad_maximum_fusion.2), channel_id=1, source_target_pairs={{0,8},{4,12},{8,16},{12,20},{16,24},{20,28},{1,9},{5,13},{9,17},{1... | collective-permute-start | bytes 405512 | tf_op jit(solution)/shard_map/ppermute | solution.py:66
  38.8 1.0 collective-permute-done.1
  39.8 7.7 %collective-permute-start.3 = (bf16[528,128]{1,0:T(8,128)(2,1)}, bf16[528,128]{1,0:T(8,128)(2,1)}, u32[]{:S(2)}, u32[]{:S(2)}) collective-permute-start(bf16[528,128]{1,0:T(8,128)(2,1)} %pad_maximum_fusion.2), channel_id=1, source_target_pairs={{0,24},{4,28},{1,25},{5,29},{2,26},{6,30},{3,27},{7,31}} | collective-permute-start | bytes 405512 | tf_op jit(solution)/shard_map/ppermute | solution.py:66
  49.7 1.3 select_convert_fusion
  51.1 1.0 collective-permute-start.4
  53.9 1.2 collective-permute-start.12
  56.0 1.1 collective-permute-start.11
  59.2 1.7 fusion.48
  60.9 1.6 copy.84
  64.5 1.9 fusion.41
  67.0 1.1 collective-permute-start.16
  68.2 0.9 collective-permute-start.14
  69.1 2.3 collective-permute-done.11
  71.4 2.3 collective-permute-start.15
  73.7 1.8 fusion.38
  76.0 2.4 collective-permute-done.16
  78.4 2.3 collective-permute-start.18
  80.7 5.0 %collective-permute-done.13 = bf16[176,1024]{1,0:T(8,128)(2,1)} collective-permute-done((bf16[176,1024]{1,0:T(8,128)(2,1)}, bf16[176,1024]{1,0:T(8,128)(2,1)}, u32[]{:S(2)}, u32[]{:S(2)}) %collective-permute-start.13) | collective-permute-done | bytes 360480 | tf_op jit(solution)/shard_map/ppermute | solution.py:24
  86.0 1.7 fusion.35
  88.2 2.8 collective-permute-done.18
  91.1 2.6 collective-permute-done.17
  93.7 1.5 convolution_convert_fusion.2
  109.0 1.6 collective-permute-start.20
  115.8 4.7 %collective-permute-done.20 = bf16[1,8,64,336]{3,2,0,1:T(8,128)(2,1)S(1)} collective-permute-done((bf16[1,8,64,336]{3,2,0,1:T(8,128)(2,1)S(1)}, bf16[1,8,64,336]{3,2,0,1:T(8,128)(2,1)S(1)}, u32[]{:S(2)}, u32[]{:S(2)}) %collective-permute-start.20) | collective-permute-done | bytes 344096 | tf_op jit(solution)/shard_map/ppermute | solution.py:116
  122.3 68.2 %all_to_all.10 = bf16[32,16,2688]{2,1,0:T(8,128)(2,1)S(1)} all-to-all(bf16[32,16,2688]{2,1,0:T(8,128)(2,1)S(1)} %bitcast.201), channel_id=1, replica_groups=mesh['grp'=1,'seq'=8,'head'=4] {'seq','head'}, dimensions={0} | all-to-all | bytes 5505024 | tf_op jit(solution)/shard_map/all_to_all | solution.py:292
  190.6 5.0 %collective-permute-done.21 = bf16[32,16,2688]{2,1,0:T(8,128)(2,1)S(1)} collective-permute-done((bf16[32,16,2688]{2,1,0:T(8,128)(2,1)S(1)}, bf16[32,16,2688]{2,1,0:T(8,128)(2,1)S(1)}, u32[]{:S(2)}, u32[]{:S(2)}) %collective-permute-start.21) | collective-permute-done | bytes 2752544 | tf_op jit(solution)/shard_map/ppermute | solution.py:123
  195.6 2.9 pad_maximum_fusion
  198.5 18.9 %convolution_convert_fusion = bf16[1024,2688]{1,0:T(8,128)(2,1)} fusion(bf16[1,928,2688]{2,1,0:T(8,128)(2,1)} %param.38, bf16[1024,2688]{1,0:T(8,128)(2,1)} %bitcast.200, bf16[1,2688,928]{1,2,0:T(8,128)(2,1)} %param.37), kind=kOutput, calls=%fused_computation.1 | convolution fusion | flops 10222927872 | bytes 20987904 | tf_op jit(solution)/shard_map/dot_general | solution.py:132
  217.4 2.1 slice.233
  219.7 5.0 %collective-permute-done.22 = bf16[32,16,2688]{2,1,0:T(8,128)(2,1)S(1)} collective-permute-done((bf16[32,16,2688]{2,1,0:T(8,128)(2,1)S(1)}, bf16[32,16,2688]{2,1,0:T(8,128)(2,1)S(1)}, u32[]{:S(2)}, u32[]{:S(2)}) %collective-permute-start.22) | collective-permute-done | bytes 2752544 | tf_op jit(solution)/shard_map/ppermute | solution.py:123
  224.7 2.2 add_convert_fusion
  226.9 3.7 %all-to-all-start.1 = ((bf16[32,16,2688]{2,1,0:T(8,128)(2,1)}), bf16[32,16,2688]{2,1,0:T(8,128)(2,1)S(1)}, u32[]{:S(2)}, u32[]{:S(2)}) async-start(bf16[32,16,2688]{2,1,0:T(8,128)(2,1)} %add_convert_fusion), calls=%async_computation.1 | async-start | bytes 5505024 | tf_op jit(solution)/shard_map/all_to_all | solution.py:300
  231.1 62.2 %all-to-all-done.1 = bf16[32,16,2688]{2,1,0:T(8,128)(2,1)S(1)} async-done(((bf16[32,16,2688]{2,1,0:T(8,128)(2,1)}), bf16[32,16,2688]{2,1,0:T(8,128)(2,1)S(1)}, u32[]{:S(2)}, u32[]{:S(2)}) %all-to-all-start.1) | async-done | bytes 2752544 | tf_op jit(solution)/shard_map/all_to_all | solution.py:300
  293.4 3.4 %gather_fusion = bf16[384,2688]{1,0:T(8,128)(2,1)} fusion(bf16[512,2688]{1,0:T(8,128)(2,1)S(1)} %bitcast.197, s32[1024]{0:T(1024)S(1)} %pad_clamp_fusion), kind=kCustom, calls=%fused_computation | custom fusion | bytes 4130304 | tf_op jit(solution)/shard_map/gather | solution.py:304
  296.8 4.6 %reshape.514 = f32[64,6,2688]{2,1,0:T(8,128)} reshape(bf16[384,2688]{1,0:T(8,128)(2,1)} %gather_fusion) | data formatting | bytes 6193152 | tf_op jit(solution)/shard_map/convert_element_type | solution.py:307
  301.4 4.6 %multiply_reduce_fusion = f32[64,2688]{1,0:T(8,128)S(1)} fusion(f32[64,6,2688]{2,1,0:T(8,128)} %reshape.514, f32[64,6]{1,0:T(8,128)S(1)} %copy.95), kind=kLoop, calls=%fused_computation.3 | loop fusion | flops 1892352 | bytes 4818432 | tf_op jit(solution)/shard_map/reduce_sum | solution.py:307
  (177 shorter events, 26.0 us)
Async XLA Ops:
  0.0 12.6 %copy-start = (bf16[256,256]{1,0:T(8,128)(2,1)S(1)}, bf16[256,256]{1,0:T(8,128)(2,1)}, u32[]{:S(2)}) copy-start(bf16[256,256]{1,0:T(8,128)(2,1)} %param.26) | copy-start | bytes 393220
  1.8 52.2 %collective-permute-start.8 = (bf16[160,1024]{1,0:T(8,128)(2,1)}, bf16[160,1024]{1,0:T(8,128)(2,1)}, u32[]{:S(2)}, u32[]{:S(2)}) collective-permute-start(bf16[160,1024]{1,0:T(8,128)(2,1)} %slice.224), channel_id=1, source_target_pairs={{0,4},{8,0},{16,8},{24,16},{28,24},{20,28},{12,20},{4,12},{1,5},{9... | collective-permute-start | bytes 983048 | tf_op jit(solution)/shard_map/ppermute | solution.py:24
  4.8 50.4 %collective-permute-start.6 = (bf16[160,1024]{1,0:T(8,128)(2,1)}, bf16[160,1024]{1,0:T(8,128)(2,1)}, u32[]{:S(2)}, u32[]{:S(2)}) collective-permute-start(bf16[160,1024]{1,0:T(8,128)(2,1)} %slice.224), channel_id=1, source_target_pairs={{0,8},{8,16},{16,24},{24,28},{28,20},{20,12},{12,4},{4,0},{1,9},{9... | collective-permute-start | bytes 983048 | tf_op jit(solution)/shard_map/ppermute | solution.py:24
  6.6 49.5 %collective-permute-start.7 = (bf16[176,1024]{1,0:T(8,128)(2,1)}, bf16[176,1024]{1,0:T(8,128)(2,1)}, u32[]{:S(2)}, u32[]{:S(2)}) collective-permute-start(bf16[176,1024]{1,0:T(8,128)(2,1)} %slice.223), channel_id=1, source_target_pairs={{0,4},{8,0},{16,8},{24,16},{28,24},{20,28},{12,20},{4,12},{1,5},{9... | collective-permute-start | bytes 1081352 | tf_op jit(solution)/shard_map/ppermute | solution.py:24
  8.5 48.6 %collective-permute-start.5 = (bf16[176,1024]{1,0:T(8,128)(2,1)}, bf16[176,1024]{1,0:T(8,128)(2,1)}, u32[]{:S(2)}, u32[]{:S(2)}) collective-permute-start(bf16[176,1024]{1,0:T(8,128)(2,1)} %slice.223), channel_id=1, source_target_pairs={{0,8},{8,16},{16,24},{24,28},{28,20},{20,12},{12,4},{4,0},{1,9},{9... | collective-permute-start | bytes 1081352 | tf_op jit(solution)/shard_map/ppermute | solution.py:24
  12.6 4.2 %copy-start.11 = (bf16[256,256]{1,0:T(8,128)(2,1)S(1)}, bf16[256,256]{1,0:T(8,128)(2,1)}, u32[]{:S(2)}) copy-start(bf16[256,256]{1,0:T(8,128)(2,1)} %param.27) | copy-start | bytes 393220
  13.9 3.2 %copy-start.12 = (f32[256,16]{0,1:T(8,128)S(1)}, f32[256,16]{0,1:T(8,128)}, u32[]{:S(2)}) copy-start(f32[256,16]{0,1:T(8,128)} %param.28) | copy-start | bytes 49156
  14.8 10.0 %collective-permute-start = (bf16[528,128]{1,0:T(8,128)(2,1)S(1)}, bf16[528,128]{1,0:T(8,128)(2,1)S(1)}, u32[]{:S(2)}, u32[]{:S(2)}) collective-permute-start(bf16[528,128]{1,0:T(8,128)(2,1)S(1)} %pad_maximum_fusion.1), channel_id=1, source_target_pairs={{0,4},{4,0},{8,12},{12,8},{16,20},{20,16},{24,28},{28,24},{1,5},{5... | collective-permute-start | bytes 405512 | tf_op jit(solution)/shard_map/ppermute | solution.py:54
  17.1 2.0 copy-start.21
  17.1 2.3 copy-start.8
  24.8 1.8 copy-start.17
  26.6 4.1 %collective-permute-start.2 = (bf16[528,128]{1,0:T(8,128)(2,1)}, bf16[528,128]{1,0:T(8,128)(2,1)S(1)}, u32[]{:S(2)}, u32[]{:S(2)}) collective-permute-start(bf16[528,128]{1,0:T(8,128)(2,1)} %pad_maximum_fusion.2), channel_id=1, source_target_pairs={{0,16},{4,20},{8,24},{12,28},{1,17},{5,21},{9,25},{13,29},{2,18},{... | collective-permute-start | bytes 405512 | tf_op jit(solution)/shard_map/ppermute | solution.py:66
  30.7 9.1 %collective-permute-start.1 = (bf16[528,128]{1,0:T(8,128)(2,1)}, bf16[528,128]{1,0:T(8,128)(2,1)}, u32[]{:S(2)}, u32[]{:S(2)}) collective-permute-start(bf16[528,128]{1,0:T(8,128)(2,1)} %pad_maximum_fusion.2), channel_id=1, source_target_pairs={{0,8},{4,12},{8,16},{12,20},{16,24},{20,28},{1,9},{5,13},{9,17},{1... | collective-permute-start | bytes 405512 | tf_op jit(solution)/shard_map/ppermute | solution.py:66
  37.6 0.5 copy-start.19
  39.8 9.9 %collective-permute-start.3 = (bf16[528,128]{1,0:T(8,128)(2,1)}, bf16[528,128]{1,0:T(8,128)(2,1)}, u32[]{:S(2)}, u32[]{:S(2)}) collective-permute-start(bf16[528,128]{1,0:T(8,128)(2,1)} %pad_maximum_fusion.2), channel_id=1, source_target_pairs={{0,24},{4,28},{1,25},{5,29},{2,26},{6,30},{3,27},{7,31}} | collective-permute-start | bytes 405512 | tf_op jit(solution)/shard_map/ppermute | solution.py:66
  48.3 0.6 copy-start.20
  49.6 9.6 %copy-start.10 = (f32[256,1024]{0,1:T(8,128)S(1)}, f32[256,1024]{0,1:T(8,128)}, u32[]{:S(2)}) copy-start(f32[256,1024]{0,1:T(8,128)} %copy.85) | copy-start | bytes 3145732
  49.6 9.6 %copy-start.15 = (f32[256,16]{0,1:T(8,128)S(1)}, f32[256,16]{0,1:T(8,128)}, u32[]{:S(2)}) copy-start(f32[256,16]{0,1:T(8,128)} %get-tuple-element.146) | copy-start | bytes 49156
  49.6 9.6 %copy-start.22 = (f32[16]{0:T(128)S(1)}, f32[16]{0:T(128)}, u32[]{:S(2)}) copy-start(f32[16]{0:T(128)} %param.30) | copy-start | bytes 196
  51.1 7.0 %collective-permute-start.4 = (bf16[512,128]{1,0:T(8,128)(2,1)S(1)}, bf16[512,128]{1,0:T(8,128)(2,1)S(1)}, u32[]{:S(2)}, u32[]{:S(2)}) collective-permute-start(bf16[512,128]{1,0:T(8,128)(2,1)S(1)} %select_convert_fusion), channel_id=1, source_target_pairs={{0,4},{4,0},{8,12},{12,8},{16,20},{20,16},{24,28},{28,24},{1,5},{5... | collective-permute-start | bytes 393224 | tf_op jit(solution)/shard_map/ppermute | solution.py:81
  53.9 13.1 %collective-permute-start.12 = (bf16[160,1024]{1,0:T(8,128)(2,1)}, bf16[160,1024]{1,0:T(8,128)(2,1)}, u32[]{:S(2)}, u32[]{:S(2)}) collective-permute-start(bf16[160,1024]{1,0:T(8,128)(2,1)} %collective-permute-done.8), channel_id=1, source_target_pairs={{0,4},{8,0},{16,8},{24,16},{28,24},{20,28},{12,20},{4,12},{1,5},{9... | collective-permute-start | bytes 983048 | tf_op jit(solution)/shard_map/ppermute | solution.py:24
  55.1 13.1 %collective-permute-start.10 = (bf16[160,1024]{1,0:T(8,128)(2,1)}, bf16[160,1024]{1,0:T(8,128)(2,1)}, u32[]{:S(2)}, u32[]{:S(2)}) collective-permute-start(bf16[160,1024]{1,0:T(8,128)(2,1)} %collective-permute-done.6), channel_id=1, source_target_pairs={{0,8},{8,16},{16,24},{24,28},{28,20},{20,12},{12,4},{4,0},{1,9},{9... | collective-permute-start | bytes 983048 | tf_op jit(solution)/shard_map/ppermute | solution.py:24
  56.0 15.3 %collective-permute-start.11 = (bf16[176,1024]{1,0:T(8,128)(2,1)}, bf16[176,1024]{1,0:T(8,128)(2,1)}, u32[]{:S(2)}, u32[]{:S(2)}) collective-permute-start(bf16[176,1024]{1,0:T(8,128)(2,1)} %collective-permute-done.7), channel_id=1, source_target_pairs={{0,4},{8,0},{16,8},{24,16},{28,24},{20,28},{12,20},{4,12},{1,5},{9... | collective-permute-start | bytes 1081352 | tf_op jit(solution)/shard_map/ppermute | solution.py:24
  57.1 16.6 %collective-permute-start.9 = (bf16[176,1024]{1,0:T(8,128)(2,1)}, bf16[176,1024]{1,0:T(8,128)(2,1)}, u32[]{:S(2)}, u32[]{:S(2)}) collective-permute-start(bf16[176,1024]{1,0:T(8,128)(2,1)} %collective-permute-done.5), channel_id=1, source_target_pairs={{0,8},{8,16},{16,24},{24,28},{28,20},{20,12},{12,4},{4,0},{1,9},{9... | collective-permute-start | bytes 1081352 | tf_op jit(solution)/shard_map/ppermute | solution.py:24
  60.9 2.4 copy-start.9
  60.9 2.3 copy-start.18
  63.0 1.1 copy-start.7
  67.0 11.4 %collective-permute-start.16 = (bf16[160,1024]{1,0:T(8,128)(2,1)}, bf16[160,1024]{1,0:T(8,128)(2,1)}, u32[]{:S(2)}, u32[]{:S(2)}) collective-permute-start(bf16[160,1024]{1,0:T(8,128)(2,1)} %collective-permute-done.12), channel_id=1, source_target_pairs={{0,4},{8,0},{16,8},{24,16},{28,24},{20,28},{12,20},{4,12},{1,5},{9... | collective-permute-start | bytes 983048 | tf_op jit(solution)/shard_map/ppermute | solution.py:24
  68.2 17.5 %collective-permute-start.14 = (bf16[160,1024]{1,0:T(8,128)(2,1)}, bf16[160,1024]{1,0:T(8,128)(2,1)}, u32[]{:S(2)}, u32[]{:S(2)}) collective-permute-start(bf16[160,1024]{1,0:T(8,128)(2,1)} %collective-permute-done.10), channel_id=1, source_target_pairs={{0,8},{8,16},{16,24},{24,28},{28,20},{20,12},{12,4},{4,0},{1,9},{9... | collective-permute-start | bytes 983048 | tf_op jit(solution)/shard_map/ppermute | solution.py:24
  71.4 14.6 %collective-permute-start.15 = (bf16[176,1024]{1,0:T(8,128)(2,1)}, bf16[176,1024]{1,0:T(8,128)(2,1)S(1)}, u32[]{:S(2)}, u32[]{:S(2)}) collective-permute-start(bf16[176,1024]{1,0:T(8,128)(2,1)} %collective-permute-done.11), channel_id=1, source_target_pairs={{0,4},{8,0},{16,8},{24,16},{28,24},{20,28},{12,20},{4,12},{1,5},{9... | collective-permute-start | bytes 1081352 | tf_op jit(solution)/shard_map/ppermute | solution.py:24
  73.7 12.0 %collective-permute-start.13 = (bf16[176,1024]{1,0:T(8,128)(2,1)}, bf16[176,1024]{1,0:T(8,128)(2,1)}, u32[]{:S(2)}, u32[]{:S(2)}) collective-permute-start(bf16[176,1024]{1,0:T(8,128)(2,1)} %collective-permute-done.9), channel_id=1, source_target_pairs={{0,8},{8,16},{16,24},{24,28},{28,20},{20,12},{12,4},{4,0},{1,9},{9... | collective-permute-start | bytes 1081352 | tf_op jit(solution)/shard_map/ppermute | solution.py:24
  78.4 12.7 %collective-permute-start.18 = (bf16[160,1024]{1,0:T(8,128)(2,1)}, bf16[160,1024]{1,0:T(8,128)(2,1)}, u32[]{:S(2)}, u32[]{:S(2)}) collective-permute-start(bf16[160,1024]{1,0:T(8,128)(2,1)} %collective-permute-done.16), channel_id=1, source_target_pairs={{0,4},{8,0},{16,8},{24,16},{28,24},{20,28},{12,20},{4,12},{1,5},{9... | collective-permute-start | bytes 983048 | tf_op jit(solution)/shard_map/ppermute | solution.py:24
  85.7 8.0 %collective-permute-start.17 = (bf16[176,1024]{1,0:T(8,128)(2,1)}, bf16[176,1024]{1,0:T(8,128)(2,1)}, u32[]{:S(2)}, u32[]{:S(2)}) collective-permute-start(bf16[176,1024]{1,0:T(8,128)(2,1)} %collective-permute-done.13), channel_id=1, source_target_pairs={{0,8},{8,16},{16,24},{24,28},{28,20},{20,12},{12,4},{4,0},{1,9},{9... | collective-permute-start | bytes 1081352 | tf_op jit(solution)/shard_map/ppermute | solution.py:24
  88.0 18.9 %copy-start.14 = (s32[64,6]{0,1:T(8,128)S(1)}, s32[64,6]{0,1:T(8,128)}, u32[]{:S(2)}) copy-start(s32[64,6]{0,1:T(8,128)} %param.36) | copy-start | bytes 4612
  95.4 13.2 %collective-permute-start.19 = (bf16[2,8,64,336]{3,2,0,1:T(8,128)(2,1)S(1)}, bf16[2,8,64,336]{3,2,0,1:T(8,128)(2,1)S(1)}, u32[]{:S(2)}, u32[]{:S(2)}) collective-permute-start(bf16[2,8,64,336]{3,2,0,1:T(8,128)(2,1)S(1)} %dynamic-slice_bitcast_fusion), channel_id=1, source_target_pairs={{0,1},{1,0},{2,3},{3,2},{4,5},{5,4},{6,7},{7,6},{8,9},{9,8},{10,11... | collective-permute-start | bytes 2064392 | tf_op jit(solution)/shard_map/ppermute | solution.py:116
  108.9 12.1 %copy-start.5 = (bf16[64,2688]{1,0:T(8,128)(2,1)S(1)}, bf16[64,2688]{1,0:T(8,128)(2,1)}, u32[]{:S(2)}) copy-start(bf16[64,2688]{1,0:T(8,128)(2,1)} %param.33) | copy-start | bytes 1032196
  109.0 11.5 %collective-permute-start.20 = (bf16[1,8,64,336]{3,2,0,1:T(8,128)(2,1)S(1)}, bf16[1,8,64,336]{3,2,0,1:T(8,128)(2,1)S(1)}, u32[]{:S(2)}, u32[]{:S(2)}) collective-permute-start(bf16[1,8,64,336]{3,2,0,1:T(8,128)(2,1)S(1)} %constant_dynamic-slice_fusion.1), channel_id=1, source_target_pairs={{0,2},{1,3},{2,0},{3,1},{4,6},{5,7},{6,4},{7,5},{8,10},{9,11},{10,... | collective-permute-start | bytes 1032200 | tf_op jit(solution)/shard_map/ppermute | solution.py:116
  115.8 5.5 %copy-start.16 = (f32[2688]{0:T(1024)S(1)}, f32[2688]{0:T(1024)}, u32[]{:S(2)}) copy-start(f32[2688]{0:T(1024)} %param.34) | copy-start | bytes 32260
  121.0 1.3 copy-start.3
  190.5 5.1 %collective-permute-start.21 = (bf16[32,16,2688]{2,1,0:T(8,128)(2,1)S(1)}, bf16[32,16,2688]{2,1,0:T(8,128)(2,1)S(1)}, u32[]{:S(2)}, u32[]{:S(2)}) collective-permute-start(bf16[32,16,2688]{2,1,0:T(8,128)(2,1)S(1)} %all_to_all.10), channel_id=1, source_target_pairs={{0,1},{1,0},{2,3},{3,2},{4,5},{5,4},{6,7},{7,6},{8,9},{9,8},{10,11... | collective-permute-start | bytes 8257544 | tf_op jit(solution)/shard_map/ppermute | solution.py:123
  217.4 7.3 %copy-start.2 = (bf16[1024,2688]{1,0:T(8,128)(2,1)S(1)}, bf16[1024,2688]{1,0:T(8,128)(2,1)}, u32[]{:S(2)}) copy-start(bf16[1024,2688]{1,0:T(8,128)(2,1)} %convolution_convert_fusion) | copy-start | bytes 16515076
  219.5 5.2 %collective-permute-start.22 = (bf16[32,16,2688]{2,1,0:T(8,128)(2,1)S(1)}, bf16[32,16,2688]{2,1,0:T(8,128)(2,1)S(1)}, u32[]{:S(2)}, u32[]{:S(2)}) collective-permute-start(bf16[32,16,2688]{2,1,0:T(8,128)(2,1)S(1)} %slice.233), channel_id=1, source_target_pairs={{0,1},{1,0},{2,3},{3,2},{4,5},{5,4},{6,7},{7,6},{8,9},{9,8},{10,11... | collective-permute-start | bytes 8257544 | tf_op jit(solution)/shard_map/ppermute | solution.py:123
  226.9 3.9 %copy-start.13 = (bf16[2688,16]{0,1:T(8,128)(2,1)S(1)}, bf16[2688,16]{0,1:T(8,128)(2,1)}, u32[]{:S(2)}) copy-start(bf16[2688,16]{0,1:T(8,128)(2,1)} %param.35) | copy-start | bytes 258052
  226.9 66.5 %all-to-all-start.1 = ((bf16[32,16,2688]{2,1,0:T(8,128)(2,1)}), bf16[32,16,2688]{2,1,0:T(8,128)(2,1)S(1)}, u32[]{:S(2)}, u32[]{:S(2)}) async-start(bf16[32,16,2688]{2,1,0:T(8,128)(2,1)} %add_convert_fusion), calls=%async_computation.1 | async-start | bytes 5505024 | tf_op jit(solution)/shard_map/all_to_all | solution.py:300
  296.8 10.0 %copy-start.1 = (bf16[256,256]{1,0:T(8,128)(2,1)S(1)}, bf16[256,256]{1,0:T(8,128)(2,1)}, u32[]{:S(2)}) copy-start(bf16[256,256]{1,0:T(8,128)(2,1)} %param.26) | copy-start | bytes 393220
  301.4 4.6 %copy-start.4 = (f32[64,2688]{1,0:T(8,128)S(1)}, f32[64,2688]{1,0:T(8,128)}, u32[]{:S(2)}) copy-start(f32[64,2688]{1,0:T(8,128)} %copy-done.3) | copy-start | bytes 2064388
  301.4 4.6 %copy-start.6 = (bf16[64,2688]{1,0:T(8,128)(2,1)S(1)}, bf16[64,2688]{1,0:T(8,128)(2,1)}, u32[]{:S(2)}) copy-start(bf16[64,2688]{1,0:T(8,128)(2,1)} %param.33) | copy-start | bytes 1032196
